TPU v7x, 256 devices: a whole 4x4x8 slice. The times are simulated.
256 devices in a mesh: tm: 64 (over z, x, core), row: 4 (over y).
Axes of the slice: x: 4, y: 4, z: 8, core: 2. Of those that a mesh axis runs over, the one named last changes fastest.
Arguments:
- filter_map: bfloat16 [1024, 256, 256], P('tm', 'row'), may hold values from -1 to 1
- filter_cov: bfloat16 [1024, 256, 256], P('tm', 'row'), may hold values from -1 to 1
- smoother_gain: bfloat16 [1024, 256, 256], P('tm', 'row'), may hold values from -1 to 1
- transition: bfloat16 [256, 256], replicated, may hold values from -0.375 to 0.375
- site_basis: bfloat16 [2048, 256], replicated, may hold values from -0.375 to 0.375
- obs_time: int32 [32768], P('tm'), may hold values from 0 to 1023, as said below
- obs_site: int32 [32768], P('tm'), may hold values from 0 to 2047
- obs_value: float32 [32768, 128], P('tm'), may hold values from -6 to 6
- obs_weight: float32 [32768], P('tm'), may hold values from 0.5 to 8
Outputs:
- smoothed: float32 [1024, 256, 128], P('tm', 'row')
Inputs may be any that keep to these rules, and one draw needn't show every extreme that they name: `obs_time`: row r has a time step from (r // 512) * 16 to (r // 512 + 1) * 16 - 1; rows are in no order of time.
All inputs are finite; a program needn't handle non-finite values.
Results may differ from a plain program's by a relative error of at most 0.0041.
Values may be sent and summed in bfloat16 or wider, within the bound.
No kernel may reach another device: no remote copies, remote signals or barrier semaphores. Data moves between devices by JAX's collectives and lax.ppermute only.
A program may use at most 128 MiB of HBM per device.

v0:
```python
import jax
import jax.numpy as jnp
from jax import lax
from jax.sharding import PartitionSpec as P

highest = lax.Precision.HIGHEST


def entering(value, axis, join, neutral, backward):
    count, mine = (lax.axis_size(axis), lax.axis_index(axis))
    pieces = jax.tree.map(lambda part: lax.all_gather(part, axis), value)
    if backward:
        pieces = jax.tree.map(lambda part: part[::-1], pieces)
        mine = count - 1 - mine
    running = jax.tree.map(
        lambda part, zero: jnp.full_like(part, 0) + jnp.asarray(zero, part.dtype), value, neutral
    )

    def step(position, running):
        longer = join(running, jax.tree.map(lambda part: part[position], pieces))
        return jax.tree.map(lambda new, old: jnp.where(position < mine, new, old), longer, running)

    return lax.fori_loop(0, count - 1, step, running)


def product(first_factor, second_factor):
    return jnp.dot(
        first_factor, second_factor, precision=highest, preferred_element_type=jnp.float32
    )


def compose(earlier, later):
    return (product(later[0], earlier[0]), product(later[0], earlier[1]) + later[1])


def gain_at(gain_matrix, last_flag):
    return jnp.where(last_flag, jnp.zeros((), jnp.float32), gain_matrix.astype(jnp.float32))


def build_information(obs_time, obs_site, obs_value, obs_weight, site_basis, num_steps):
    local_time = obs_time - lax.axis_index("tm") * num_steps
    basis_rows = jnp.take(site_basis, obs_site, axis=0)
    weighted = (obs_weight[:, None] * obs_value).astype(jnp.bfloat16)

    def one_step(time_step_index):
        masked = jnp.where(
            (local_time == time_step_index)[:, None], basis_rows, jnp.zeros((), jnp.bfloat16)
        )
        summed = lax.dot_general(
            masked, weighted, (((0,), (0,)), ((), ())), preferred_element_type=jnp.float32
        )
        return summed.astype(jnp.bfloat16)

    return lax.map(one_step, jnp.arange(num_steps, dtype=jnp.int32))


def forward_prefix(summary, identity_pair):
    return entering((summary[0], summary[1]), "tm", compose, identity_pair, False)


def backward_prefix(summary, identity_pair):
    return entering((summary[0], summary[1]), "tm", compose, identity_pair, True)


def offset_terms(gains, mean_share, filtered, transition_wide, final_flags):

    def one_offset(running, inputs):
        gain_matrix, mean_part, mean_whole, last_flag = inputs
        pushed = product(transition_wide, mean_whole)
        corrected = mean_part - product(gain_at(gain_matrix, last_flag), pushed)
        return (running, jnp.where(last_flag, mean_part, corrected))

    return lax.scan(one_offset, 0, (gains, mean_share, filtered, final_flags))[1]


def whole_passes(maps_whole, gains_whole, drive_whole, transition_wide, final_flags, identity_pair):

    def summary_step(running, inputs):
        return (compose(running, (inputs[0].astype(jnp.float32), inputs[1])), None)

    summary = lax.scan(summary_step, identity_pair, (maps_whole, drive_whole))[0]
    incoming = forward_prefix(summary, identity_pair)

    def filter_step(current, inputs):
        current = product(inputs[0].astype(jnp.float32), current) + inputs[1]
        return (current, current)

    filtered = lax.scan(filter_step, incoming[1], (maps_whole, drive_whole))[1]
    offsets = offset_terms(gains_whole, filtered, filtered, transition_wide, final_flags)

    def smooth_summary(running, inputs):
        return (compose(running, (gain_at(inputs[0], inputs[2]), inputs[1])), None)

    back_summary = lax.scan(
        smooth_summary, identity_pair, (gains_whole, offsets, final_flags), reverse=True
    )[0]
    outgoing = backward_prefix(back_summary, identity_pair)

    def smooth_step(current, inputs):
        current = product(gain_at(inputs[0], inputs[2]), current) + inputs[1]
        return (current, current)

    return lax.scan(smooth_step, outgoing[1], (gains_whole, offsets, final_flags), reverse=True)[1]


def local(
    filter_map,
    filter_cov,
    smoother_gain,
    transition,
    site_basis,
    obs_time,
    obs_site,
    obs_value,
    obs_weight,
):
    num_steps = filter_map.shape[0]
    row_count = filter_map.shape[1]
    state_width = filter_map.shape[2]
    members = obs_value.shape[1]
    row_start = lax.axis_index("row") * row_count
    is_final = lax.axis_index("tm") == lax.axis_size("tm") - 1
    final_flags = jnp.logical_and(is_final, jnp.arange(num_steps) == num_steps - 1)
    identity = jnp.eye(state_width, dtype=jnp.float32)
    transition_wide = transition.astype(jnp.float32)
    identity_pair = (identity, jnp.zeros((state_width, members), jnp.float32))
    information = build_information(
        obs_time, obs_site, obs_value, obs_weight, site_basis, num_steps
    )
    maps_whole, gains_whole, covs_whole = (
        lax.all_gather(filter_map, "row", axis=1, tiled=True),
        lax.all_gather(smoother_gain, "row", axis=1, tiled=True),
        lax.all_gather(filter_cov, "row", axis=1, tiled=True),
    )
    drive_whole = jnp.einsum(
        "kij,kje->kie", covs_whole, information, preferred_element_type=jnp.float32
    )
    smoothed = whole_passes(
        maps_whole, gains_whole, drive_whole, transition_wide, final_flags, identity_pair
    )
    return lax.dynamic_slice_in_dim(smoothed, row_start, row_count, 1)


def solution(mesh):
    placed = (
        P("tm", "row", None),
        P("tm", "row", None),
        P("tm", "row", None),
        P(),
        P(),
        P("tm"),
        P("tm"),
        P("tm", None),
        P("tm"),
    )
    return jax.shard_map(
        local, mesh=mesh, in_specs=placed, out_specs=P("tm", "row", None), check_vma=False
    )
```

profile of v0, /device:TPU:1, one launch (start us, length us, event | category | flops | bytes accessed | tf_op | source)
XLA Modules:
  0.0 877.9 jit_solution(3602552848383626959)
XLA Ops:
  12.4 38.2 %while.106 = (s32[]{:T(128)}, bf16[16,256,128]{2,1,0:T(8,128)(2,1)}, s32[16]{0:T(128)S(1)}, s32[512]{0:T(512)S(1)}, bf16[512,256]{1,0:T(8,128)(2,1)S(1)}, /*index=5*/bf16[512,128]{1,0:T(8,128)(2,1)S(1)}, s32[]{:T(128)}) while((s32[]{:T(128)}, bf16[16,256,128]{2,1,0:T(8,128)(2,1)}, s32[16]{0:T(128)S(1)}, s32[512]{0:T(512)S(1)}, ...), condition=%wide.region_1.2_spmd, body=%wide.region_0.1_spmd.sunk | while | flops 33718784 | bytes 462429 | solution.py:54
  50.7 2.7 convolution_bitcast_fusion
  55.3 26.1 %all-gather.14.cloned.1.call-done = bf16[16,256,256]{2,1,0:T(8,128)(2,1)} async-done(((bf16[16,64,256]{2,1,0:T(8,128)(2,1)}), bf16[16,256,256]{2,1,0:T(8,128)(2,1)}) %all-gather.14.cloned.1.call-update) | async-done | bytes 2097168 | tf_op jit(solution)/shard_map/all_gather | solution.py:131
  81.4 40.7 %while.110 = (s32[]{:T(128)}, f32[256,256]{1,0:T(8,128)S(1)}, f32[256,128]{1,0:T(8,128)S(1)}, bf16[16,256,256]{2,1,0:T(8,128)(2,1)}, f32[16,256,128]{2,1,0:T(8,128)}, /*index=5*/s32[]{:T(128)}, s32[]{:T(128)}) while((s32[]{:T(128)}, f32[256,256]{1,0:T(8,128)S(1)}, f32[256,128]{1,0:T(8,128)S(1)}, bf16[16,256,256]{2,1,0:T(8,128)(2,1)}, ...), condition=%wide.region_3.4_spmd.clone, body=%wide.region_2.3_spmd.clone.sunk | while | flops 302055424 | bytes 1967703 | solution.py:81
  124.1 82.4 %all-gather.20.cloned.1.call-done = f32[16384,128]{1,0:T(8,128)} async-done(((f32[256,128]{1,0:T(8,128)}), f32[16384,128]{1,0:T(8,128)}) %all-gather.20.cloned.1.call-update) | async-done | bytes 8388624 | tf_op jit(solution)/shard_map/all_gather | solution.py:11
  206.5 98.7 %all-gather.18.cloned.1.call-done = f32[16384,256]{1,0:T(8,128)} async-done(((f32[256,256]{1,0:T(8,128)}), f32[16384,256]{1,0:T(8,128)}) %all-gather.18.cloned.1.call-update) | async-done | bytes 16777232 | tf_op jit(solution)/shard_map/all_gather | solution.py:11
  305.2 89.4 %while.111 = (s32[]{:T(128)}, f32[256,128]{1,0:T(8,128)S(1)}, s32[]{:T(128)}, f32[64,256,256]{2,1,0:T(8,128)}, f32[64,256,128]{2,1,0:T(8,128)}, /*index=5*/s32[]{:T(128)}, s32[]{:T(128)}) while((s32[]{:T(128)}, f32[256,128]{1,0:T(8,128)S(1)}, s32[]{:T(128)}, f32[64,256,256]{2,1,0:T(8,128)}, f32[64,256,128]{2,1,0:T(8,128)}, ...), condition=%wide.region_5.6_spmd.clone, body=%wide.region_4.5_spmd.clone.sunk | while | flops 100794368 | bytes 1051231 | solution.py:23
  394.7 20.7 %while.107 = (s32[]{:T(128)}, f32[256,128]{1,0:T(8,128)S(1)}, f32[16,256,128]{2,1,0:T(8,128)S(1)}, bf16[16,256,256]{2,1,0:T(8,128)(2,1)}, f32[16,256,128]{2,1,0:T(8,128)}, /*index=5*/s32[]{:T(128)}) while((s32[]{:T(128)}, f32[256,128]{1,0:T(8,128)S(1)}, f32[16,256,128]{2,1,0:T(8,128)S(1)}, bf16[16,256,256]{2,1,0:T(8,128)(2,1)}, ...), condition=%wide.region_7.8_spmd, body=%wide.region_6.7_spmd.sunk | while | flops 100696064 | bytes 918597 | solution.py:88
  417.0 57.1 %while.108 = (s32[]{:T(128)}, f32[16,256,128]{2,1,0:T(8,128)}, pred[16]{0:T(512)(128)(4,1)S(1)}, f32[16,256,128]{2,1,0:T(8,128)S(1)}, bf16[16,256,256]{2,1,0:T(8,128)(2,1)}, /*index=5*/f32[256,256]{1,0:T(8,128)S(1)}, s32[]{:T(128)}) while((s32[]{:T(128)}, f32[16,256,128]{2,1,0:T(8,128)}, pred[16]{0:T(512)(128)(4,1)S(1)}, ...), condition=%wide.region_9.10_spmd, body=%wide.region_8.9_spmd.sunk | while | flops 201523200 | bytes 1050711 | solution.py:73
  418.0 2.6 fusion.121
  421.6 2.6 fusion.121
  425.1 2.6 fusion.121
  428.7 2.6 fusion.121
  432.3 2.6 fusion.121
  435.9 2.6 fusion.121
  439.4 2.6 fusion.121
  443.0 2.6 fusion.121
  446.6 2.6 fusion.121
  450.2 2.6 fusion.121
  453.7 2.6 fusion.121
  457.3 2.6 fusion.121
  460.8 2.6 fusion.121
  464.4 2.6 fusion.121
  468.0 2.6 fusion.121
  471.5 2.6 fusion.121
  474.1 73.4 %while.112 = (s32[]{:T(128)}, f32[256,256]{1,0:T(8,128)S(1)}, f32[256,128]{1,0:T(8,128)S(1)}, pred[16]{0:T(512)(128)(4,1)S(1)}, bf16[16,256,256]{2,1,0:T(8,128)(...) while((s32[]{:T(128)}, f32[256,256]{1,0:T(8,128)S(1)}, ...), condition=%wide.region_11.12_spmd.clone, body=%wide.region_10.11_spmd.clone.sunk | while | flops 302317568 | bytes 1968764 | solution.py:94
  549.0 79.4 %all-gather.24.cloned.1.call-done = f32[16384,128]{1,0:T(8,128)} async-done(((f32[256,128]{1,0:T(8,128)}), f32[16384,128]{1,0:T(8,128)}) %all-gather.24.cloned.1.call-update) | async-done | bytes 8388624 | tf_op jit(solution)/shard_map/all_gather | solution.py:11
  628.3 7.6 rev.7
  636.0 91.2 %all-gather.22.cloned.1.call-done = f32[16384,256]{1,0:T(8,128)} async-done(((f32[256,256]{1,0:T(8,128)}), f32[16384,256]{1,0:T(8,128)}) %all-gather.22.cloned.1.call-update) | async-done | bytes 16777232 | tf_op jit(solution)/shard_map/all_gather | solution.py:11
  727.2 11.5 %rev.6 = f32[64,256,256]{2,1,0:T(8,128)} reverse(f32[64,256,256]{2,1,0:T(8,128)} %bitcast.136), dimensions={0} | reverse | bytes 33554432 | tf_op jit(solution)/shard_map/rev | solution.py:13
  738.7 89.4 %while.113 = (s32[]{:T(128)}, f32[256,128]{1,0:T(8,128)S(1)}, s32[]{:T(128)}, f32[64,256,256]{2,1,0:T(8,128)}, f32[64,256,128]{2,1,0:T(8,128)}, /*index=5*/s32[]{:T(128)}, s32[]{:T(128)}) while((s32[]{:T(128)}, f32[256,128]{1,0:T(8,128)S(1)}, s32[]{:T(128)}, f32[64,256,256]{2,1,0:T(8,128)}, f32[64,256,128]{2,1,0:T(8,128)}, ...), condition=%wide.region_13.14_spmd.clone, body=%wide.region_12.13_spmd.clone.sunk | while | flops 100794368 | bytes 1051231 | solution.py:23
  828.3 41.9 %while.109 = (s32[]{:T(128)}, f32[256,128]{1,0:T(8,128)S(1)}, f32[16,256,128]{2,1,0:T(8,128)S(1)}, pred[16]{0:T(512)(128)(4,1)S(1)}, bf16[16,256,256]{2,1,0:T(8,...) while((s32[]{:T(128)}, f32[256,128]{1,0:T(8,128)S(1)}, f32[16,256,128]{2,1,0:T(8,128)S(1)}, ...), condition=%wide.region_15.16_spmd, body=%wide.region_14.15_spmd.sunk | while | flops 100827136 | bytes 919143 | solution.py:103
  (612 shorter events, 416.1 us)
Async XLA Ops:
  6.5 3.6 copy-start
  6.5 5.7 copy-start.6
  6.5 5.7 copy-start.8
  6.5 44.1 %all-gather.16.cloned.1.call-start = ((), (), s32[]{:S(2)}) async-start(), calls=%async_computation.2 | async-start | bytes 2621440 | tf_op jit(solution)/shard_map/all_gather | solution.py:133
  7.3 74.1 %all-gather.14.cloned.1.call-start = ((), (), s32[]{:S(2)}) async-start(), calls=%async_computation.1 | async-start | bytes 2621440 | tf_op jit(solution)/shard_map/all_gather | solution.py:131
  8.0 198.5 %all-gather.20.cloned.1.call-start = ((), (), s32[]{:S(2)}) async-start(), calls=%async_computation.4 | async-start | bytes 8519680 | tf_op jit(solution)/shard_map/all_gather | solution.py:11
  81.4 42.6 %copy-start.7 = (bf16[256,256]{1,0:T(8,128)(2,1)S(1)}, bf16[256,256]{1,0:T(8,128)(2,1)}, u32[]{:S(2)}) copy-start(bf16[256,256]{1,0:T(8,128)(2,1)} %param.28) | copy-start | bytes 393220
  122.1 0.7 copy-start.5
  122.1 0.7 copy-start.3
  122.8 182.4 %all-gather.18.cloned.1.call-start = ((), (), s32[]{:S(2)}) async-start(), calls=%async_computation.3 | async-start | bytes 17039360 | tf_op jit(solution)/shard_map/all_gather | solution.py:11
  123.4 292.1 %all-gather.12.cloned.1.call-start = ((), (), s32[]{:S(2)}) async-start(), calls=%async_computation | async-start | bytes 2621440 | tf_op jit(solution)/shard_map/all_gather | solution.py:132
  123.9 504.4 %all-gather.24.cloned.1.call-start = ((), (), s32[]{:S(2)}) async-start(), calls=%async_computation.6 | async-start | bytes 8519680 | tf_op jit(solution)/shard_map/all_gather | solution.py:11
  547.5 0.7 copy-start.4
  547.6 0.7 copy-start.2
  548.2 178.9 %all-gather.22.cloned.1.call-start = ((), (), s32[]{:S(2)}) async-start(), calls=%async_computation.5 | async-start | bytes 17039360 | tf_op jit(solution)/shard_map/all_gather | solution.py:11
  828.3 42.8 %copy-start.1 = (bf16[2048,256]{1,0:T(8,128)(2,1)S(1)}, bf16[2048,256]{1,0:T(8,128)(2,1)}, u32[]{:S(2)}) copy-start(bf16[2048,256]{1,0:T(8,128)(2,1)} %param.29) | copy-start | bytes 3145732
Sparse Core Ops, SparseCore 0:
  9.1 36.9 all-gather.15
  48.0 33.3 all-gather.13
  122.9 83.5 all-gather.19
  209.1 96.0 all-gather.17
  306.8 29.7 all-gather.11
  548.3 79.9 all-gather.23
  631.1 96.0 all-gather.21
where the time goes:
time: 883 us; the launch traced here: 878 us
  matrix products  394 us (45%)
  waiting for transfers between devices  381 us (43%)
  local copies, waits for them, and re-layouts  68.6 us (8%)
  between operations  13.8 us (2%)
  other arithmetic  13.5 us (2%)
    dot_general x254, matrix products, product(): jnp.dot(first_factor, second_factor, precision=highest, preferred_element...  375 us
    all_gather x4, waiting for transfers between devices, entering(): pieces = jax.tree.map(lambda part: lax.all_gather(part, axis), value)  352 us
    dynamic_slice x48, local copies, waits for them, and re-layouts, offset_terms(): lax.scan(one_offset, 0, (gains, mean_share, filtered, final_flags))[1]  28.3 us
    all_gather x1, waiting for transfers between devices, local(): lax.all_gather(filter_map, 'row', axis=1, tiled=True)  26.1 us
    rev x2, local copies, waits for them, and re-layouts, entering(): pieces = jax.tree.map(lambda part: part[::-1], pieces)  19.1 us
  transfers between devices with their start and end apart: 7, of which 5 were waited for; matrix products, arithmetic and copies ran while one was open for 18% of the time, Pallas kernels for 0%

commit v1 on v0

v1 whole, which is shorter than its diff:
```python
import jax
import jax.numpy as jnp
from jax import lax
from jax.experimental import pallas as pl
from jax.experimental.pallas import tpu as pltpu
from jax.sharding import Mesh, PartitionSpec as P

BF = jnp.bfloat16
F32 = jnp.float32
NZ, NX, NC, NR = 8, 4, 2, 4
NT = (((1,), (1,)), ((), ()))
VM = pl.BlockSpec(memory_space=pltpu.VMEM)
HB = pl.BlockSpec(memory_space=pltpu.HBM)
SM = pl.BlockSpec(memory_space=pltpu.SMEM)


def split(value):
    hi = value.astype(BF)
    return hi, (value - hi.astype(F32)).astype(BF)


def mm(left, right):
    return jnp.dot(left, right, preferred_element_type=F32)


def mm3(left_hi, left_lo, right_hi, right_lo):
    return mm(left_hi, right_hi) + (mm(left_hi, right_lo) + mm(left_lo, right_hi))


def push(state, weight):
    hi, lo = split(state)
    both = lax.dot_general(
        jnp.concatenate([hi, lo], axis=0), weight, NT, preferred_element_type=F32
    )
    n = state.shape[0]
    return both[:n] + both[n:]


def push2(state, weight_hi, weight_lo):
    hi, lo = split(state)
    both = lax.dot_general(
        jnp.concatenate([hi, lo], axis=0), weight_hi, NT, preferred_element_type=F32
    )
    n = state.shape[0]
    extra = lax.dot_general(hi, weight_lo, NT, preferred_element_type=F32)
    return both[:n] + (both[n:] + extra)


def coords(idx_ref):
    me = idx_ref[0]
    row = me % NR
    tm = me // NR
    return tm // (NX * NC), (tm // NC) % NX, tm % NC, row


def call(body, outs, *args, scratch=(), far_in=(), far_out=()):
    many = isinstance(outs, tuple)
    count = len(outs) if many else 1
    specs = tuple(HB if i in far_out else VM for i in range(count))
    far = len(far_in) + len(far_out)
    if many:
        outs = tuple(
            pltpu.HBM(o.shape, o.dtype) if i in far_out else o for i, o in enumerate(outs)
        )
    args = [args[0]] + [
        pltpu.with_memory_space_constraint(a, pltpu.HBM) if i in far_in else a
        for i, a in enumerate(args[1:])
    ]
    return pl.pallas_call(
        body,
        out_shape=outs,
        in_specs=[SM] + [HB if i in far_in else VM for i in range(len(args) - 1)],
        out_specs=specs if many else specs[0],
        scratch_shapes=list(scratch) + ([pltpu.SemaphoreType.DMA((far,))] if far else []),
        compiler_params=pltpu.CompilerParams(vmem_limit_bytes=16 << 20),
    )(*args)


def shape(dims, dtype):
    return jax.ShapeDtypeStruct(dims, dtype)


def drive_body(idx, basis, value, weight, time, cov, *outs):
    row = idx[0] % NR
    steps = cov.shape[0]
    weighted = (weight[...] * jnp.transpose(value[...])).astype(BF)
    local_time = time[...] - (idx[0] // NR) * steps
    half = steps // 2
    members = weighted.shape[0] // NR
    for k in range(steps):
        masked = jnp.where(local_time == k, weighted, jnp.zeros((), BF))
        info = mm(masked, basis[...]).astype(BF)
        drive = lax.dot_general(info, cov[k], NT, preferred_element_type=F32)
        w = drive.shape[1]
        lane = (k // half) * w
        for s, out in enumerate(outs):
            part = drive[0:members]
            for r in range(1, NR):
                part = jnp.where((row + s) % NR == r, drive[r * members : (r + 1) * members], part)
            out[k % half, :, lane : lane + w] = part


def assemble(row, parts, full):
    w = parts[0].shape[1]
    for s, part in enumerate(parts):
        start = pl.multiple_of(((row - s) % NR) * w, w)
        full[:, pl.ds(start, w), :] = part[...]


def tree(items, order):
    while len(items) > 1:
        merged = []
        for i in range(0, len(items), 2):
            left, right = order(items[i], items[i + 1])
            if left[1] is None:
                value = mm(left[0], right[0])
            else:
                value = mm3(left[0], left[1], right[0], right[1])
            merged.append(split(value))
        items = merged
    return items[0]


def later_first(a, b):
    return b, a


def earlier_first(a, b):
    return a, b


def fwd_local_body(idx, m0, m1, m2, m3, full, packed):
    _, _, _, row = coords(idx)
    assemble(row, (m0, m1, m2, m3), full)
    steps, n = full.shape[0], full.shape[1]
    hi, lo = tree([(full[k], None) for k in range(steps)], later_first)
    packed[0:n] = hi
    packed[n:] = lo


def fwd_drive_body(idx, full, d0, d1, d2, d3, far_full, far_drives, msg, drv, drives, sems):
    _, _, _, row = coords(idx)
    save_full = pltpu.make_async_copy(full, far_full, sems.at[0])
    save_full.start()
    for s, part in enumerate((d0, d1, d2, d3)):
        drv[(row - s) % NR] = part[...]
    steps, n = full.shape[0], full.shape[1]
    half, w = steps // 2, n // NR
    for k in range(steps):
        lane = (k // half) * w
        drives[k] = jnp.concatenate(
            [drv[r, k % half, :, lane : lane + w] for r in range(NR)], axis=1
        )
    save_drives = pltpu.make_async_copy(drives, far_drives, sems.at[1])
    save_drives.start()
    b = drives[0]
    for k in range(1, steps):
        b = push(b, full[k]) + drives[k]
    store_pair(msg, b)
    save_full.wait()
    save_drives.wait()


def store_pair(msg, b):
    m = b.shape[0]
    hi, lo = split(b)
    msg[0:m] = hi
    msg[m:] = lo


def load_pair(msg):
    m = msg.shape[0] // 2
    return msg[0:m].astype(F32) + msg[m:].astype(F32)


def fwd_core_body(idx, own, other, b_own, b_other, far_other, far_b, keep, msg, sems):
    save_other = pltpu.make_async_copy(other, far_other, sems.at[0])
    save_b = pltpu.make_async_copy(b_other, far_b, sems.at[1])
    save_other.start()
    save_b.start()
    _, _, c, _ = coords(idx)
    n = own.shape[1]
    m = b_own.shape[0] // 2
    first = jnp.where(c == 0, own[...], other[...])
    second = jnp.where(c == 0, other[...], own[...])
    hi, lo = split(mm3(second[0:n], second[n:], first[0:n], first[n:]))
    b_mine, b_theirs = load_pair(b_own), load_pair(b_other)
    b_first = jnp.where(c == 0, b_mine, b_theirs)
    b_second = jnp.where(c == 0, b_theirs, b_mine)
    b = push2(b_first, second[0:n], second[n:]) + b_second
    w = n // NC
    keep[0:n] = hi
    keep[n : 2 * n] = lo
    b_hi, b_lo = split(b)
    keep[2 * n : 2 * n + m] = b_hi
    keep[2 * n + m :] = b_lo
    msg[0:n] = half_of(c, hi, w)
    msg[n : 2 * n] = half_of(c, lo, w)
    msg[2 * n :] = pack_vector(c, b)
    save_other.wait()
    save_b.wait()


def half_of(c, value, w):
    return jnp.where(c == 0, value[:, :w], value[:, w:])


def pack_vector(c, b):
    m, n = b.shape
    w, q = n // NC, m // NC
    hi, lo = split(jnp.where(c == 0, b[:q], b[q:]))
    return jnp.concatenate([hi[:, :w], hi[:, w:], lo[:, :w], lo[:, w:]], axis=0)


def unpack_part(msg, at, q):
    p = [msg[at + j * q : at + (j + 1) * q].astype(F32) for j in range(4)]
    return jnp.concatenate([p[0] + p[2], p[1] + p[3]], axis=1)


def unpack_vector(c, mine, other, at, m):
    q = m // NC
    a, b = unpack_part(mine, at, q), unpack_part(other, at, q)
    return jnp.concatenate([jnp.where(c == 0, a, b), jnp.where(c == 0, b, a)], axis=0)


def join(c, mine, other, rows):
    a, b = mine[0:rows], other[0:rows]
    return jnp.concatenate([jnp.where(c == 0, a, b), jnp.where(c == 0, b, a)], axis=1)


def fwd_x_body(idx, own, r1, r2, r3, s1, s2, s3, far_ax, far_bx, msg, ax, bx, sems):
    _, x, c, _ = coords(idx)
    rows, n = ax.shape[1:]
    m = bx.shape[1]
    for s, (mine, other) in enumerate(((own, None), (r1, s1), (r2, s2), (r3, s3))):
        at = (x - s) % NX
        if other is None:
            ax[at] = mine[0:rows]
            bx[at] = mine[rows : rows + m].astype(F32) + mine[rows + m :].astype(F32)
        else:
            ax[at] = join(c, mine, other, rows)
            bx[at] = unpack_vector(c, mine, other, rows, m)
    save_ax = pltpu.make_async_copy(ax, far_ax, sems.at[0])
    save_bx = pltpu.make_async_copy(bx, far_bx, sems.at[1])
    save_ax.start()
    save_bx.start()
    hi, _ = tree([(ax[i, 0:n], ax[i, n:]) for i in range(NX)], later_first)
    b = bx[0]
    for i in range(1, NX):
        b = push2(b, ax[i, 0:n], ax[i, n:]) + bx[i]
    hi = half_of(c, hi, n // NC)
    packed = pack_vector(c, b)
    for i in range(NZ):
        msg[i, 0:n] = hi
        msg[i, n:] = packed
    save_ax.wait()
    save_bx.wait()


def bwd_local_body(idx, g0, g1, g2, g3, far_full, packed, full, sems):
    _, _, _, row = coords(idx)
    assemble(row, (g0, g1, g2, g3), full)
    steps, n = full.shape[0], full.shape[1]

    @pl.when(idx[0] // NR == NZ * NX * NC - 1)
    def _():
        full[steps - 1] = jnp.zeros((n, n), BF)

    save_full = pltpu.make_async_copy(full, far_full, sems.at[0])
    save_full.start()
    hi, lo = tree([(full[k], None) for k in range(steps)], earlier_first)
    packed[0:n] = hi
    packed[n:] = lo
    save_full.wait()


def bwd_core_body(idx, own, other, out):
    _, _, c, _ = coords(idx)
    n = own.shape[1]
    first = jnp.where(c == 0, own[...], other[...])
    second = jnp.where(c == 0, other[...], own[...])
    hi, lo = split(mm3(first[0:n], first[n:], second[0:n], second[n:]))
    out[0:n] = hi
    out[n:] = lo


def bwd_x_body(idx, m0, m1, m2, m3, far_cx, msg, cx, sems):
    _, x, c, _ = coords(idx)
    n = cx.shape[2]
    for s, part in enumerate((m0, m1, m2, m3)):
        cx[(x - s) % NX] = part[...]
    save_cx = pltpu.make_async_copy(cx, far_cx, sems.at[0])
    save_cx.start()
    hi, _ = tree([(cx[i, 0:n], cx[i, n:]) for i in range(NX)], earlier_first)
    hi = half_of(c, hi, n // NC)
    for i in range(NZ):
        msg[i] = hi
    save_cx.wait()


def load(sems, at, *pairs):
    copies = []
    for i, (far, close) in enumerate(pairs):
        copy = pltpu.make_async_copy(far, close, sems.at[at + i])
        copy.start()
        copies.append(copy)
    return copies


def fetch_body(idx, far, out, sems):
    copy = pltpu.make_async_copy(far, out, sems.at[0])
    copy.start()
    copy.wait()


def filter_body(
    idx, mine, swapped, b_other, far_other, far_transition, far_ax, far_bx, far_full, far_drives, far_gains,
    far_off, msg, other, transition, ax, bx, full, drives, gains, off, sems,
):
    z, x, c, _ = coords(idx)
    steps, n = full.shape[0], full.shape[1]
    m = drives.shape[1]
    get_ax, get_bx, get_other, get_drives, get_full, get_gains, get_transition = load(
        sems, 0, (far_ax, ax), (far_bx, bx), (far_other, other), (far_drives, drives),
        (far_full, full), (far_gains, gains), (far_transition, transition),
    )
    state = jnp.zeros((m, n), F32)
    for i in range(NZ - 1):
        b = unpack_vector(c, mine.at[i], swapped.at[i], n, m)
        moved = push(state, join(c, mine.at[i], swapped.at[i], n)) + b
        state = jnp.where(i < z, moved, state)
    get_ax.wait()
    get_bx.wait()
    for i in range(NX - 1):
        moved = push2(state, ax[i, 0:n], ax[i, n:]) + bx[i]
        state = jnp.where(i < x, moved, state)
    get_other.wait()
    moved = push2(state, other[0:n], other[n:]) + load_pair(b_other)
    state = jnp.where(c == 1, moved, state)
    get_drives.wait()
    get_full.wait()
    for k in range(steps):
        state = push(state, full[k]) + drives[k]
        drives[k] = state
    get_gains.wait()
    get_transition.wait()
    weight = transition[...]
    for k in range(steps):
        mean = drives[k]
        off[k] = mean - push(push(mean, weight), gains[k])
    save_off = pltpu.make_async_copy(off, far_off, sems.at[7])
    save_off.start()
    f = off[steps - 1]
    for k in range(steps - 2, -1, -1):
        f = push(f, gains[k]) + off[k]
    store_pair(msg, f)
    save_off.wait()


def back_core_body(idx, own, other, cown, cother, out):
    _, _, c, _ = coords(idx)
    n = own.shape[1]
    f_own, f_other = load_pair(own), load_pair(other)
    f0 = jnp.where(c == 0, f_own, f_other)
    f1 = jnp.where(c == 0, f_other, f_own)
    hi = jnp.where(c == 0, cown[0:n], cother[0:n])
    lo = jnp.where(c == 0, cown[n:], cother[n:])
    out[...] = push2(f1, hi, lo) + f0


def back_x_body(idx, f0, f1, f2, f3, far_cx, fx, out, cx, sems):
    (get_cx,) = load(sems, 0, (far_cx, cx))
    _, x, _, _ = coords(idx)
    n = fx.shape[2]
    for s, part in enumerate((f0, f1, f2, f3)):
        fx[(x - s) % NX] = part[...]
    get_cx.wait()
    f = fx[NX - 1]
    for i in range(NX - 2, -1, -1):
        f = push2(f, cx[i, 0:n], cx[i, n:]) + fx[i]
    for i in range(NZ):
        out[i] = f


def smooth_body(
    idx, mine, swapped, fz, fx, fother, cother, far_cx, far_gains, far_off, o0, o1, o2, o3,
    cx, gains, off, sems,
):
    get_cx, get_gains, get_off = load(
        sems, 0, (far_cx, cx), (far_gains, gains), (far_off, off)
    )
    z, x, c, row = coords(idx)
    steps, n = gains.shape[0], gains.shape[1]
    m = off.shape[1]
    half, w = steps // 2, n // NR
    state = jnp.zeros((m, n), F32)
    for i in range(NZ - 1, 0, -1):
        moved = push(state, join(c, mine.at[i], swapped.at[i], n)) + fz[i].astype(F32)
        state = jnp.where(i > z, moved, state)
    get_cx.wait()
    for i in range(NX - 1, 0, -1):
        moved = push2(state, cx[i, 0:n], cx[i, n:]) + fx[i]
        state = jnp.where(i > x, moved, state)
    moved = push2(state, cother[0:n], cother[n:]) + load_pair(fother)
    state = jnp.where(c == 0, moved, state)
    get_gains.wait()
    get_off.wait()
    for k in range(steps - 1, -1, -1):
        state = push(state, gains[k]) + off[k]
        lane = (k // half) * w
        parts = [state[:, r * w : (r + 1) * w].astype(BF) for r in range(NR)]
        for s, out in enumerate((o0, o1, o2, o3)):
            part = parts[0]
            for r in range(1, NR):
                part = jnp.where((row + s) % NR == r, parts[r], part)
            out[k % half, :, lane : lane + w] = part


def place_body(idx, p0, p1, p2, p3, out, got):
    _, _, _, row = coords(idx)
    half = out.shape[0] // 2
    w = out.shape[1]
    for s, part in enumerate((p0, p1, p2, p3)):
        got[(row - s) % NR] = part[...]
    for k in range(half):
        block = jnp.concatenate([got[r, k] for r in range(NR)], axis=0).astype(F32)
        turned = jnp.transpose(block)
        out[k] = turned[:w]
        out[k + half] = turned[w:]


def shift(value, axis, step, size):
    return lax.ppermute(value, axis, [(i, (i + step) % size) for i in range(size)])


def spread(value, axis):
    return lax.all_to_all(value, axis, 0, 0, tiled=True)


def swap(value):
    return lax.ppermute(value, "c", [(0, 1), (1, 0)])


def gather_rows(value):
    return [value] + [shift(value, "row", s, NR) for s in range(1, NR)]


def local(
    filter_map,
    filter_cov,
    smoother_gain,
    transition,
    site_basis,
    obs_time,
    obs_site,
    obs_value,
    obs_weight,
):
    steps, w, n = filter_map.shape
    obs, members = obs_value.shape
    m = members // NR
    half = steps // 2
    tm = (lax.axis_index("z") * NX + lax.axis_index("x")) * NC + lax.axis_index("c")
    idx = (tm * NR + lax.axis_index("row")).astype(jnp.int32).reshape(1)

    maps = gather_rows(filter_map)
    basis_rows = site_basis.at[obs_site].get(mode="promise_in_bounds")
    drive = call(
        drive_body,
        (shape((half, m, 2 * w), F32),) * NR,
        idx,
        basis_rows,
        obs_value,
        obs_weight.reshape(1, obs),
        obs_time.reshape(1, obs),
        filter_cov,
    )
    gain_in, _ = lax.optimization_barrier((smoother_gain, drive))
    drive = drive[:1] + tuple(shift(drive[s], "row", s, NR) for s in range(1, NR))
    gains = gather_rows(gain_in)
    full, packed = call(
        fwd_local_body,
        (shape((steps, n, n), BF), shape((2 * n, n), BF)),
        idx,
        *maps,
    )
    packed_other = swap(packed)
    full, drives, bmsg = call(
        fwd_drive_body,
        (shape((steps, n, n), BF), shape((steps, m, n), F32), shape((2 * m, n), BF)),
        idx,
        full,
        *drive,
        scratch=[pltpu.VMEM((NR, half, m, 2 * w), F32), pltpu.VMEM((steps, m, n), F32)],
        far_out=(0, 1),
    )
    bmsg_other = swap(bmsg)
    far_other, far_b, keep, msg = call(
        fwd_core_body,
        (
            shape((2 * n, n), BF),
            shape((2 * m, n), BF),
            shape((2 * n + 2 * m, n), BF),
            shape((2 * n + 2 * m, n // NC), BF),
        ),
        idx,
        packed,
        packed_other,
        bmsg,
        bmsg_other,
        far_out=(0, 1),
    )
    got = [shift(msg, "x", s, NX) for s in range(1, NX)]
    ax, bx, msg = call(
        fwd_x_body,
        (
            shape((NX, 2 * n, n), BF),
            shape((NX, m, n), F32),
            shape((NZ, n + 2 * m, n // NC), BF),
        ),
        idx,
        keep,
        *got,
        *[swap(g) for g in got],
        scratch=[pltpu.VMEM((NX, 2 * n, n), BF), pltpu.VMEM((NX, m, n), F32)],
        far_out=(0, 1),
    )
    up = spread(msg, "z")

    gains, _ = lax.optimization_barrier((gains, msg))
    gfull, cpacked = call(
        bwd_local_body, (shape((steps, n, n), BF), shape((2 * n, n), BF)), idx, *gains,
        scratch=[pltpu.VMEM((steps, n, n), BF)],
        far_out=(0,),
    )
    cother = swap(cpacked)
    c32 = call(bwd_core_body, shape((2 * n, n), BF), idx, cpacked, cother)
    got = [shift(c32, "x", s, NX) for s in range(1, NX)]
    cx, cmsg = call(
        bwd_x_body,
        (shape((NX, 2 * n, n), BF), shape((NZ, n, n // NC), BF)),
        idx,
        c32,
        *got,
        scratch=[pltpu.VMEM((NX, 2 * n, n), BF)],
        far_out=(0,),
    )
    down = spread(cmsg, "z")
    b_other = call(fetch_body, shape((2 * m, n), BF), idx, far_b, far_in=(0,))
    off, fmsg = call(
        filter_body,
        (shape((steps, m, n), F32), shape((2 * m, n), BF)),
        idx,
        up,
        swap(up),
        b_other,
        far_other,
        transition,
        ax,
        bx,
        full,
        drives,
        gfull,
        scratch=[
            pltpu.VMEM((2 * n, n), BF),
            pltpu.VMEM((n, n), BF),
            pltpu.VMEM((NX, 2 * n, n), BF),
            pltpu.VMEM((NX, m, n), F32),
            pltpu.VMEM((steps, n, n), BF),
            pltpu.VMEM((steps, m, n), F32),
            pltpu.VMEM((steps, n, n), BF),
            pltpu.VMEM((steps, m, n), F32),
        ],
        far_in=(3, 4, 5, 6, 7, 8, 9),
        far_out=(0,),
    )
    fother = swap(fmsg)
    f = call(back_core_body, shape((m, n), F32), idx, fmsg, fother, cpacked, cother)
    fx, f = call(
        back_x_body,
        (shape((NX, m, n), F32), shape((NZ, m, n), F32)),
        idx,
        f,
        *[shift(f, "x", s, NX) for s in range(1, NX)],
        cx,
        scratch=[pltpu.VMEM((NX, 2 * n, n), BF)],
        far_in=(4,),
    )
    fz = spread(f, "z")
    out = call(
        smooth_body,
        (shape((half, m, 2 * w), BF),) * NR,
        idx,
        down,
        swap(down),
        fz,
        fx,
        fother,
        cother,
        cx,
        gfull,
        off,
        scratch=[
            pltpu.VMEM((NX, 2 * n, n), BF),
            pltpu.VMEM((steps, n, n), BF),
            pltpu.VMEM((steps, m, n), F32),
        ],
        far_in=(6, 7, 8),
    )
    out = out[:1] + tuple(shift(out[s], "row", s, NR) for s in range(1, NR))
    return call(
        place_body,
        shape((steps, w, members), F32),
        idx,
        *out,
        scratch=[pltpu.VMEM((NR, half, m, 2 * w), BF)],
    )


def solution(mesh):
    fine = Mesh(mesh.devices.reshape(NZ, NX, NC, NR), ("z", "x", "c", "row"))
    t = ("z", "x", "c")
    placed = (
        P(t, "row", None),
        P(t, "row", None),
        P(t, "row", None),
        P(),
        P(),
        P(t),
        P(t),
        P(t, None),
        P(t),
    )

    return jax.shard_map(
        local, mesh=fine, in_specs=placed, out_specs=P(t, "row", None), check_vma=False
    )
```

time: 883 us -> 196 us (0.22)
  matrix products: 394 us -> 0 us
  waiting for transfers between devices: 381 us -> 88.3 us
  starting transfers between devices: 0.24 us -> 60 us
  local copies, waits for them, and re-layouts: 68.6 us -> 10.5 us
  Pallas kernels: 0 us -> 33.9 us
  between operations: 13.8 us -> 0.21 us
  other arithmetic: 13.5 us -> 0.69 us
    dot_general x271 -> x0, matrix products: 394 us -> none  [the longest x254 375 us: product(): jnp.dot(first_factor, second_factor, precision=highest, preferred_element...]
    all_gather x7 -> x0, waiting for transfers between devices: 378 us -> none  [the longest x4 352 us: entering(): pieces = jax.tree.map(lambda part: lax.all_gather(part, axis), value)]
    ppermute x0 -> x30, waiting for transfers between devices: none -> 73.9 us  [the longest x21 69.6 us: shift(): lax.ppermute(value, axis, [(i, (i + step) % size) for i in range(size)])]
    ppermute x0 -> x30, starting transfers between devices: none -> 41.7 us  [the longest x21 30.4 us: shift(): lax.ppermute(value, axis, [(i, (i + step) % size) for i in range(size)])]
    dynamic_slice x65 -> x0, local copies, waits for them, and re-layouts: 39.8 us -> none  [the longest x48 28.3 us: offset_terms(): lax.scan(one_offset, 0, (gains, mean_share, filtered, final_flags))[1]]
    pallas_call x0 -> x14, Pallas kernels: none -> 33.9 us  [call(): pl.pallas_call(body, out_shape=outs, in_specs=[SM] + [HB if i in far_in e...]
    rev x2 -> x0, local copies, waits for them, and re-layouts: 19.1 us -> none  [entering(): pieces = jax.tree.map(lambda part: part[::-1], pieces)]
    all_to_all x0 -> x3, starting transfers between devices: none -> 18.2 us  [spread(): return lax.all_to_all(value, axis, 0, 0, tiled=True)]
  transfers between devices with their start and end apart: 7 -> 33, of which waited for: 5 -> 25; matrix products, arithmetic and copies ran while one was open for 18% -> 1% of each run, Pallas kernels for 0% -> 11%
where the time goes in v1:
time: 196 us; the launch traced here: 194 us
  waiting for transfers between devices  88.3 us (45%)
  starting transfers between devices  60 us (31%)
  Pallas kernels  33.9 us (17%)
  local copies, waits for them, and re-layouts  10.5 us (5%)
    ppermute x21, waiting for transfers between devices, shift(): lax.ppermute(value, axis, [(i, (i + step) % size) for i in range(size)])  69.6 us
    pallas_call x14, Pallas kernels, call(): pl.pallas_call(body, out_shape=outs, in_specs=[SM] + [HB if i in far_in e...  33.9 us
    ppermute x21, starting transfers between devices, shift(): lax.ppermute(value, axis, [(i, (i + step) % size) for i in range(size)])  30.4 us
    all_to_all x3, starting transfers between devices, spread(): return lax.all_to_all(value, axis, 0, 0, tiled=True)  18.2 us
    all_to_all x3, waiting for transfers between devices, spread(): return lax.all_to_all(value, axis, 0, 0, tiled=True)  14.3 us
    ppermute x9, starting transfers between devices, swap(): return lax.ppermute(value, 'c', [(0, 1), (1, 0)])  11.3 us
    unnamed x26, local copies, waits for them, and re-layouts  8.58 us
    ppermute x9, waiting for transfers between devices, swap(): return lax.ppermute(value, 'c', [(0, 1), (1, 0)])  4.35 us
  transfers between devices with their start and end apart: 33, of which 25 were waited for; matrix products, arithmetic and copies ran while one was open for 1% of the time, Pallas kernels for 11%

profile of v1, /device:TPU:1, one launch (start us, length us, event | category | flops | bytes accessed | tf_op | source)
XLA Modules:
  0.0 193.5 jit_solution(12539854021136281389)
XLA Ops:
  0.0 2.1 %collective-permute-start.3 = (bf16[16,64,256]{2,1,0:T(8,128)(2,1)}, bf16[16,64,256]{2,1,0:T(8,128)(2,1)S(1)}, u32[]{:S(2)}, u32[]{:S(2)}) collective-permute-start(bf16[16,64,256]{2,1,0:T(8,128)(2,1)} %m0.1), channel_id=1, source_target_pairs={{0,1},{1,2},{2,3},{3,0},{4,5},{5,6},{6,7},{7,4},{8,9},{9,10},{10,1... | collective-permute-start | bytes 1572872 | tf_op jit(solution)/shard_map/ppermute | solution.py:433
  2.1 2.6 %collective-permute-start.4 = (bf16[16,64,256]{2,1,0:T(8,128)(2,1)}, bf16[16,64,256]{2,1,0:T(8,128)(2,1)S(1)}, u32[]{:S(2)}, u32[]{:S(2)}) collective-permute-start(bf16[16,64,256]{2,1,0:T(8,128)(2,1)} %m0.1), channel_id=1, source_target_pairs={{0,2},{1,3},{2,0},{3,1},{4,6},{5,7},{6,4},{7,5},{8,10},{9,11},{10,... | collective-permute-start | bytes 1572872 | tf_op jit(solution)/shard_map/ppermute | solution.py:433
  6.5 7.0 %collective-permute-done.3.m1 = bf16[16,64,256]{2,1,0:T(8,128)(2,1)S(1)} collective-permute-done((bf16[16,64,256]{2,1,0:T(8,128)(2,1)}, bf16[16,64,256]{2,1,0:T(8,128)(2,1)S(1)}, u32[]{:S(2)}, u32[]{:S(2)}) %collective-permute-start.3) | collective-permute-done | bytes 524320 | tf_op jit(solution)/shard_map/ppermute | solution.py:433
  14.3 13.3 %collective-permute-done.4.m2 = bf16[16,64,256]{2,1,0:T(8,128)(2,1)S(1)} collective-permute-done((bf16[16,64,256]{2,1,0:T(8,128)(2,1)}, bf16[16,64,256]{2,1,0:T(8,128)(2,1)S(1)}, u32[]{:S(2)}, u32[]{:S(2)}) %collective-permute-start.4) | collective-permute-done | bytes 524320 | tf_op jit(solution)/shard_map/ppermute | solution.py:433
  33.3 2.3 %shard_map.92 = (bf16[16,256,256]{2,1,0:T(8,128)(2,1)S(1)}, bf16[512,256]{1,0:T(8,128)(2,1)}) custom-call(s32[1]{0:T(128)} %bitcast.idx, bf16[16,64,256]{2,1,0:T(8,128)(2,1)S(1)} %copy-done.1, bf16[16,64,256]{2,1,0:T(8,128)(2,1)S(1)} %copy-done.4, bf16[16,64,256]{2,1,0:T(8,128)(2,1)S(1)} %copy-done.6, bf16[16,64,256]{2,1,0:T(8,128)(2,1)S(1)} %copy-done.8), custom_call_target="tpu_custom_call" | custom-call | tf_op jit(solution)/shard_map/pallas_call | solution.py:69
  37.2 2.0 %gather_fusion = bf16[512,256]{1,0:T(8,128)(2,1)S(1)} fusion(bf16[2048,256]{1,0:T(8,128)(2,1)S(1)} %copy-done, s32[1024]{0:T(1024)S(1)} %pad_clamp_fusion), kind=kCustom, calls=%fused_computation | custom fusion | bytes 526336 | tf_op jit(solution)/shard_map/gather | solution.py:467
  41.2 3.1 %shard_map.91 = (f32[8,32,128]{2,1,0:T(8,128)S(1)}, f32[8,32,128]{2,1,0:T(8,128)S(1)}, f32[8,32,128]{2,1,0:T(8,128)S(1)}, f32[8,32,128]{2,1,0:T(8,128)S(1)}) custom-call(s32[1]{0:T(128)} %bitcast.idx, bf16[512,256]{1,0:T(8,128)(2,1)S(1)} %gather_fusion, f32[512,128]{1,0:T(8,128)S(1)} %copy-done.10, f32[1,512]{1,0:T(1,128)S(1)} %bitcast.3, ...), custom_call_target="tpu_custom_call" | custom-call | tf_op jit(solution)/shard_map/pallas_call | solution.py:69
  44.6 2.1 %collective-permute-start.8 = (f32[8,32,128]{2,1,0:T(8,128)S(1)}, f32[8,32,128]{2,1,0:T(8,128)S(1)}, u32[]{:S(2)}, u32[]{:S(2)}) collective-permute-start(f32[8,32,128]{2,1,0:T(8,128)S(1)} %get-tuple-element.40), channel_id=1, source_target_pairs={{0,2},{1,3},{2,0},{3,1},{4,6},{5,7},{6,4},{7,5},{8,10},{9,11},{10,... | collective-permute-start | bytes 393224 | tf_op jit(solution)/shard_map/ppermute | solution.py:433
  48.0 3.1 %collective-permute-done.7.d1 = f32[8,32,128]{2,1,0:T(8,128)S(1)} collective-permute-done((f32[8,32,128]{2,1,0:T(8,128)S(1)}, f32[8,32,128]{2,1,0:T(8,128)S(1)}, u32[]{:S(2)}, u32[]{:S(2)}) %collective-permute-start.7) | collective-permute-done | bytes 131104 | tf_op jit(solution)/shard_map/ppermute | solution.py:433
  51.1 2.0 %collective-permute-done.8.d2 = f32[8,32,128]{2,1,0:T(8,128)S(1)} collective-permute-done((f32[8,32,128]{2,1,0:T(8,128)S(1)}, f32[8,32,128]{2,1,0:T(8,128)S(1)}, u32[]{:S(2)}, u32[]{:S(2)}) %collective-permute-start.8) | collective-permute-done | bytes 131104 | tf_op jit(solution)/shard_map/ppermute | solution.py:433
  53.8 2.7 %shard_map.93 = (bf16[16,256,256]{2,1,0:T(8,128)(2,1)}, f32[16,32,256]{2,1,0:T(8,128)}, bf16[64,256]{1,0:T(8,128)(2,1)S(1)}) custom-call(s32[1]{0:T(128)} %bitcast.idx, bf16[16,256,256]{2,1,0:T(8,128)(2,1)S(1)} %get-tuple-element.44.full, f32[8,32,128]{2,1,0:T(8,128)S(1)} %get-tuple-element.38.d0, f32[8,32,128]{2,1,0:T(8,128)S(1)} %collective-permute-done.7.d1, ...), custom_call_target="tpu_custom_call" | custom-call | tf_op jit(solution)/shard_map/pallas_call | solution.py:69
  61.7 2.4 %collective-permute-start.12 = (bf16[576,128]{1,0:T(8,128)(2,1)S(1)}, bf16[576,128]{1,0:T(8,128)(2,1)S(1)}, u32[]{:S(2)}, u32[]{:S(2)}) collective-permute-start(bf16[576,128]{1,0:T(8,128)(2,1)S(1)} %get-tuple-element.47), channel_id=1, source_target_pairs={{0,16},{8,24},{16,0},{24,8},{1,17},{9,25},{17,1},{25,9},{2,18},{10... | collective-permute-start | bytes 442376 | tf_op jit(solution)/shard_map/ppermute | solution.py:433
  68.0 2.9 %collective-permute-done.12.r2 = bf16[576,128]{1,0:T(8,128)(2,1)S(1)} collective-permute-done((bf16[576,128]{1,0:T(8,128)(2,1)S(1)}, bf16[576,128]{1,0:T(8,128)(2,1)S(1)}, u32[]{:S(2)}, u32[]{:S(2)}) %collective-permute-start.12) | collective-permute-done | bytes 147488 | tf_op jit(solution)/shard_map/ppermute | solution.py:433
  73.5 2.3 %shard_map.95 = (bf16[4,512,256]{2,1,0:T(8,128)(2,1)}, f32[4,32,256]{2,1,0:T(8,128)}, bf16[8,320,128]{2,1,0:T(8,128)(2,1)}) custom-call(s32[1]{0:T(128)} %bitcast.idx, bf16[576,256]{1,0:T(8,128)(2,1)S(1)} %get-tuple-element.46.own, bf16[576,128]{1,0:T(8,128)(2,1)S(1)} %collective-permute-done.11.r1, bf16[576,128]{1,0:T(8,128)(2,1)S(1)} %collective-permute-done.12.r2, ...), custom_call_target="tpu_custom_call" | custom-call | tf_op jit(solution)/shard_map/pallas_call | solution.py:69
  75.8 8.2 %all-to-all-start.1 = ((bf16[8,320,128]{2,1,0:T(8,128)(2,1)}), bf16[8,320,128]{2,1,0:T(8,128)(2,1)S(1)}, u32[]{:S(2)}, u32[]{:S(2)}) async-start(bf16[8,320,128]{2,1,0:T(8,128)(2,1)} %get-tuple-element.48), calls=%async_computation.1 | async-start | bytes 1310720 | tf_op jit(solution)/shard_map/all_to_all | solution.py:437
  85.0 2.7 %collective-permute-start.1 = (bf16[16,64,256]{2,1,0:T(8,128)(2,1)S(1)}, bf16[16,64,256]{2,1,0:T(8,128)(2,1)S(1)}, u32[]{:S(2)}, u32[]{:S(2)}) collective-permute-start(bf16[16,64,256]{2,1,0:T(8,128)(2,1)S(1)} %copy-done.2), channel_id=1, source_target_pairs={{0,2},{1,3},{2,0},{3,1},{4,6},{5,7},{6,4},{7,5},{8,10},{9,11},{10,... | collective-permute-start | bytes 1572872 | tf_op jit(solution)/shard_map/ppermute | solution.py:433
  87.7 10.6 %collective-permute-done.g1 = bf16[16,64,256]{2,1,0:T(8,128)(2,1)S(1)} collective-permute-done((bf16[16,64,256]{2,1,0:T(8,128)(2,1)S(1)}, bf16[16,64,256]{2,1,0:T(8,128)(2,1)S(1)}, u32[]{:S(2)}, u32[]{:S(2)}) %collective-permute-start) | collective-permute-done | bytes 524320 | tf_op jit(solution)/shard_map/ppermute | solution.py:433
  98.3 12.1 %collective-permute-done.1.g2 = bf16[16,64,256]{2,1,0:T(8,128)(2,1)S(1)} collective-permute-done((bf16[16,64,256]{2,1,0:T(8,128)(2,1)S(1)}, bf16[16,64,256]{2,1,0:T(8,128)(2,1)S(1)}, u32[]{:S(2)}, u32[]{:S(2)}) %collective-permute-start.1) | collective-permute-done | bytes 524320 | tf_op jit(solution)/shard_map/ppermute | solution.py:433
  115.9 2.1 %collective-permute-start.19 = (bf16[512,256]{1,0:T(8,128)(2,1)S(1)}, bf16[512,256]{1,0:T(8,128)(2,1)S(1)}, u32[]{:S(2)}, u32[]{:S(2)}) collective-permute-start(bf16[512,256]{1,0:T(8,128)(2,1)S(1)} %shard_map.97.m0), channel_id=1, source_target_pairs={{0,16},{8,24},{16,0},{24,8},{1,17},{9,25},{17,1},{25,9},{2,18},{10... | collective-permute-start | bytes 786440 | tf_op jit(solution)/shard_map/ppermute | solution.py:433
  119.3 4.6 %collective-permute-done.18.m1 = bf16[512,256]{1,0:T(8,128)(2,1)S(1)} collective-permute-done((bf16[512,256]{1,0:T(8,128)(2,1)S(1)}, bf16[512,256]{1,0:T(8,128)(2,1)S(1)}, u32[]{:S(2)}, u32[]{:S(2)}) %collective-permute-start.18) | collective-permute-done | bytes 262176 | tf_op jit(solution)/shard_map/ppermute | solution.py:433
  123.9 5.7 %collective-permute-done.19.m2 = bf16[512,256]{1,0:T(8,128)(2,1)S(1)} collective-permute-done((bf16[512,256]{1,0:T(8,128)(2,1)S(1)}, bf16[512,256]{1,0:T(8,128)(2,1)S(1)}, u32[]{:S(2)}, u32[]{:S(2)}) %collective-permute-start.19) | collective-permute-done | bytes 262176 | tf_op jit(solution)/shard_map/ppermute | solution.py:433
  131.8 6.6 %all-to-all-start = ((bf16[8,256,128]{2,1,0:T(8,128)(2,1)}), bf16[8,256,128]{2,1,0:T(8,128)(2,1)S(1)}, u32[]{:S(2)}, u32[]{:S(2)}) async-start(bf16[8,256,128]{2,1,0:T(8,128)(2,1)} %get-tuple-element.54), calls=%async_computation | async-start | bytes 1048576 | tf_op jit(solution)/shard_map/all_to_all | solution.py:437
  141.9 7.8 %shard_map.100 = (f32[16,32,256]{2,1,0:T(8,128)}, bf16[64,256]{1,0:T(8,128)(2,1)S(1)}) custom-call(s32[1]{0:T(128)} %bitcast.idx, bf16[8,320,128]{2,1,0:T(8,128)(2,1)S(1)} %all-to-all-done.1.mine, bf16[8,320,128]{2,1,0:T(8,128)(2,1)S(1)} %collective-permute-done.22.swapped, bf16[64,256]{1,0:T(8,128)(2,1)S(1)} %shard_map.99.b_other, ...), custom_call_target="tpu_custom_call" | custom-call | tf_op jit(solution)/shard_map/pallas_call | solution.py:69
  150.2 4.2 %all-to-all-done.mine = bf16[8,256,128]{2,1,0:T(8,128)(2,1)S(1)} async-done(((bf16[8,256,128]{2,1,0:T(8,128)(2,1)}), bf16[8,256,128]{2,1,0:T(8,128)(2,1)S(1)}, u32[]{:S(2)}, u32[]{:S(2)}) %all-to-all-start) | async-done | bytes 524320 | tf_op jit(solution)/shard_map/all_to_all | solution.py:437
  154.4 2.4 %collective-permute-start.21 = (bf16[8,256,128]{2,1,0:T(8,128)(2,1)S(1)}, bf16[8,256,128]{2,1,0:T(8,128)(2,1)S(1)}, u32[]{:S(2)}, u32[]{:S(2)}) collective-permute-start(bf16[8,256,128]{2,1,0:T(8,128)(2,1)S(1)} %all-to-all-done.mine), channel_id=1, source_target_pairs={{0,4},{4,0},{1,5},{5,1},{2,6},{6,2},{3,7},{7,3},{8,12},{12,8},{9,1... | collective-permute-start | bytes 1572872 | tf_op jit(solution)/shard_map/ppermute | solution.py:441
  157.0 2.5 %collective-permute-start.24 = (f32[32,256]{1,0:T(8,128)S(1)}, f32[32,256]{1,0:T(8,128)S(1)}, u32[]{:S(2)}, u32[]{:S(2)}) collective-permute-start(f32[32,256]{1,0:T(8,128)S(1)} %shard_map.101.f0), channel_id=1, source_target_pairs={{0,8},{8,16},{16,24},{24,0},{1,9},{9,17},{17,25},{25,1},{2,10},{10... | collective-permute-start | bytes 98312 | tf_op jit(solution)/shard_map/ppermute | solution.py:433
  159.5 2.2 %collective-permute-start.25 = (f32[32,256]{1,0:T(8,128)S(1)}, f32[32,256]{1,0:T(8,128)S(1)}, u32[]{:S(2)}, u32[]{:S(2)}) collective-permute-start(f32[32,256]{1,0:T(8,128)S(1)} %shard_map.101.f0), channel_id=1, source_target_pairs={{0,16},{8,24},{16,0},{24,8},{1,17},{9,25},{17,1},{25,9},{2,18},{10... | collective-permute-start | bytes 98312 | tf_op jit(solution)/shard_map/ppermute | solution.py:433
  164.7 2.5 %shard_map.102 = (f32[4,32,256]{2,1,0:T(8,128)S(1)}, f32[8,32,256]{2,1,0:T(8,128)}) custom-call(s32[1]{0:T(128)} %bitcast.idx, f32[32,256]{1,0:T(8,128)S(1)} %shard_map.101.f0, f32[32,256]{1,0:T(8,128)S(1)} %collective-permute-done.24.f1, f32[32,256]{1,0:T(8,128)S(1)} %collective-permute-done.25.f2, f32[32,256]{1,0:T(8,128)S(1)} %collective-permute-done.26.f3, ...), custom_call_target="tpu_custom_call" | custom-call | tf_op jit(solution)/shard_map/pallas_call | solution.py:69
  167.3 3.4 %all-to-all-start.2 = ((f32[8,32,256]{2,1,0:T(8,128)}), f32[8,32,256]{2,1,0:T(8,128)S(1)}, u32[]{:S(2)}, u32[]{:S(2)}) async-start(f32[8,32,256]{2,1,0:T(8,128)} %get-tuple-element.64), calls=%async_computation.2 | async-start | bytes 524288 | tf_op jit(solution)/shard_map/all_to_all | solution.py:437
  170.7 10.1 %all-to-all-done.2.fz = f32[8,32,256]{2,1,0:T(8,128)S(1)} async-done(((f32[8,32,256]{2,1,0:T(8,128)}), f32[8,32,256]{2,1,0:T(8,128)S(1)}, u32[]{:S(2)}, u32[]{:S(2)}) %all-to-all-start.2) | async-done | bytes 262176 | tf_op jit(solution)/shard_map/all_to_all | solution.py:437
  180.8 5.3 %shard_map.103 = (bf16[8,32,128]{2,1,0:T(8,128)(2,1)S(1)}, bf16[8,32,128]{2,1,0:T(8,128)(2,1)S(1)}, bf16[8,32,128]{2,1,0:T(8,128)(2,1)S(1)}, bf16[8,32,128]{2,1,0:T(8,128)(2,1)S(1)}) custom-call(s32[1]{0:T(128)} %bitcast.idx, bf16[8,256,128]{2,1,0:T(8,128)(2,1)S(1)} %all-to-all-done.mine, bf16[8,256,128]{2,1,0:T(8,128)(2,1)S(1)} %collective-permute-done.21.swapped, ...), custom_call_target="tpu_custom_call" | custom-call | tf_op jit(solution)/shard_map/pallas_call | solution.py:69
  186.7 2.7 %collective-permute-start.28 = (bf16[8,32,128]{2,1,0:T(8,128)(2,1)S(1)}, bf16[8,32,128]{2,1,0:T(8,128)(2,1)S(1)}, u32[]{:S(2)}, u32[]{:S(2)}) collective-permute-start(bf16[8,32,128]{2,1,0:T(8,128)(2,1)S(1)} %get-tuple-element.69), channel_id=1, source_target_pairs={{0,2},{1,3},{2,0},{3,1},{4,6},{5,7},{6,4},{7,5},{8,10},{9,11},{10,... | collective-permute-start | bytes 196616 | tf_op jit(solution)/shard_map/ppermute | solution.py:433
  (77 shorter events, 47.4 us)
Async XLA Ops:
  0.0 13.5 %collective-permute-start.3 = (bf16[16,64,256]{2,1,0:T(8,128)(2,1)}, bf16[16,64,256]{2,1,0:T(8,128)(2,1)S(1)}, u32[]{:S(2)}, u32[]{:S(2)}) collective-permute-start(bf16[16,64,256]{2,1,0:T(8,128)(2,1)} %m0.1), channel_id=1, source_target_pairs={{0,1},{1,2},{2,3},{3,0},{4,5},{5,6},{6,7},{7,4},{8,9},{9,10},{10,1... | collective-permute-start | bytes 1572872 | tf_op jit(solution)/shard_map/ppermute | solution.py:433
  2.1 25.4 %collective-permute-start.4 = (bf16[16,64,256]{2,1,0:T(8,128)(2,1)}, bf16[16,64,256]{2,1,0:T(8,128)(2,1)S(1)}, u32[]{:S(2)}, u32[]{:S(2)}) collective-permute-start(bf16[16,64,256]{2,1,0:T(8,128)(2,1)} %m0.1), channel_id=1, source_target_pairs={{0,2},{1,3},{2,0},{3,1},{4,6},{5,7},{6,4},{7,5},{8,10},{9,11},{10,... | collective-permute-start | bytes 1572872 | tf_op jit(solution)/shard_map/ppermute | solution.py:433
  4.7 23.6 %collective-permute-start.5 = (bf16[16,64,256]{2,1,0:T(8,128)(2,1)}, bf16[16,64,256]{2,1,0:T(8,128)(2,1)S(1)}, u32[]{:S(2)}, u32[]{:S(2)}) collective-permute-start(bf16[16,64,256]{2,1,0:T(8,128)(2,1)} %m0.1), channel_id=1, source_target_pairs={{0,3},{1,0},{2,1},{3,2},{4,7},{5,4},{6,5},{7,6},{8,11},{9,8},{10,9... | collective-permute-start | bytes 1572872 | tf_op jit(solution)/shard_map/ppermute | solution.py:433
  35.7 23.0 %collective-permute-start.6 = (bf16[512,256]{1,0:T(8,128)(2,1)}, bf16[512,256]{1,0:T(8,128)(2,1)}, u32[]{:S(2)}, u32[]{:S(2)}) collective-permute-start(bf16[512,256]{1,0:T(8,128)(2,1)} %get-tuple-element.43.own), channel_id=1, source_target_pairs={{0,4},{4,0},{1,5},{5,1},{2,6},{6,2},{3,7},{7,3},{8,12},{12,8},{9,1... | collective-permute-start | bytes 786440 | tf_op jit(solution)/shard_map/ppermute | solution.py:441
  44.3 6.8 %collective-permute-start.7 = (f32[8,32,128]{2,1,0:T(8,128)S(1)}, f32[8,32,128]{2,1,0:T(8,128)S(1)}, u32[]{:S(2)}, u32[]{:S(2)}) collective-permute-start(f32[8,32,128]{2,1,0:T(8,128)S(1)} %get-tuple-element.39), channel_id=1, source_target_pairs={{0,1},{1,2},{2,3},{3,0},{4,5},{5,6},{6,7},{7,4},{8,9},{9,10},{10,1... | collective-permute-start | bytes 393224 | tf_op jit(solution)/shard_map/ppermute | solution.py:433
  44.6 8.5 %collective-permute-start.8 = (f32[8,32,128]{2,1,0:T(8,128)S(1)}, f32[8,32,128]{2,1,0:T(8,128)S(1)}, u32[]{:S(2)}, u32[]{:S(2)}) collective-permute-start(f32[8,32,128]{2,1,0:T(8,128)S(1)} %get-tuple-element.40), channel_id=1, source_target_pairs={{0,2},{1,3},{2,0},{3,1},{4,6},{5,7},{6,4},{7,5},{8,10},{9,11},{10,... | collective-permute-start | bytes 393224 | tf_op jit(solution)/shard_map/ppermute | solution.py:433
  46.7 7.1 %collective-permute-start.9 = (f32[8,32,128]{2,1,0:T(8,128)S(1)}, f32[8,32,128]{2,1,0:T(8,128)S(1)}, u32[]{:S(2)}, u32[]{:S(2)}) collective-permute-start(f32[8,32,128]{2,1,0:T(8,128)S(1)} %get-tuple-element.41), channel_id=1, source_target_pairs={{0,3},{1,0},{2,1},{3,2},{4,7},{5,4},{6,5},{7,6},{8,11},{9,8},{10,9... | collective-permute-start | bytes 393224 | tf_op jit(solution)/shard_map/ppermute | solution.py:433
  56.5 2.1 %collective-permute-start.10 = (bf16[64,256]{1,0:T(8,128)(2,1)S(1)}, bf16[64,256]{1,0:T(8,128)(2,1)S(1)}, u32[]{:S(2)}, u32[]{:S(2)}) collective-permute-start(bf16[64,256]{1,0:T(8,128)(2,1)S(1)} %get-tuple-element.45.b_own), channel_id=1, source_target_pairs={{0,4},{4,0},{1,5},{5,1},{2,6},{6,2},{3,7},{7,3},{8,12},{12,8},{9,1... | collective-permute-start | bytes 98312 | tf_op jit(solution)/shard_map/ppermute | solution.py:441
  60.4 6.3 %collective-permute-start.11 = (bf16[576,128]{1,0:T(8,128)(2,1)S(1)}, bf16[576,128]{1,0:T(8,128)(2,1)S(1)}, u32[]{:S(2)}, u32[]{:S(2)}) collective-permute-start(bf16[576,128]{1,0:T(8,128)(2,1)S(1)} %get-tuple-element.47), channel_id=1, source_target_pairs={{0,8},{8,16},{16,24},{24,0},{1,9},{9,17},{17,25},{25,1},{2,10},{10... | collective-permute-start | bytes 442376 | tf_op jit(solution)/shard_map/ppermute | solution.py:433
  61.7 9.2 %collective-permute-start.12 = (bf16[576,128]{1,0:T(8,128)(2,1)S(1)}, bf16[576,128]{1,0:T(8,128)(2,1)S(1)}, u32[]{:S(2)}, u32[]{:S(2)}) collective-permute-start(bf16[576,128]{1,0:T(8,128)(2,1)S(1)} %get-tuple-element.47), channel_id=1, source_target_pairs={{0,16},{8,24},{16,0},{24,8},{1,17},{9,25},{17,1},{25,9},{2,18},{10... | collective-permute-start | bytes 442376 | tf_op jit(solution)/shard_map/ppermute | solution.py:433
  64.2 8.0 %collective-permute-start.13 = (bf16[576,128]{1,0:T(8,128)(2,1)S(1)}, bf16[576,128]{1,0:T(8,128)(2,1)S(1)}, u32[]{:S(2)}, u32[]{:S(2)}) collective-permute-start(bf16[576,128]{1,0:T(8,128)(2,1)S(1)} %get-tuple-element.47), channel_id=1, source_target_pairs={{0,24},{8,0},{16,8},{24,16},{1,25},{9,1},{17,9},{25,17},{2,26},{10... | collective-permute-start | bytes 442376 | tf_op jit(solution)/shard_map/ppermute | solution.py:433
  66.8 5.4 %collective-permute-start.14 = (bf16[576,128]{1,0:T(8,128)(2,1)S(1)}, bf16[576,128]{1,0:T(8,128)(2,1)S(1)}, u32[]{:S(2)}, u32[]{:S(2)}) collective-permute-start(bf16[576,128]{1,0:T(8,128)(2,1)S(1)} %collective-permute-done.11.r1), channel_id=1, source_target_pairs={{0,4},{4,0},{1,5},{5,1},{2,6},{6,2},{3,7},{7,3},{8,12},{12,8},{9,1... | collective-permute-start | bytes 442376 | tf_op jit(solution)/shard_map/ppermute | solution.py:441
  70.9 2.2 %collective-permute-start.15 = (bf16[576,128]{1,0:T(8,128)(2,1)S(1)}, bf16[576,128]{1,0:T(8,128)(2,1)S(1)}, u32[]{:S(2)}, u32[]{:S(2)}) collective-permute-start(bf16[576,128]{1,0:T(8,128)(2,1)S(1)} %collective-permute-done.12.r2), channel_id=1, source_target_pairs={{0,4},{4,0},{1,5},{5,1},{2,6},{6,2},{3,7},{7,3},{8,12},{12,8},{9,1... | collective-permute-start | bytes 442376 | tf_op jit(solution)/shard_map/ppermute | solution.py:441
  75.8 55.9 %all-to-all-start.1 = ((bf16[8,320,128]{2,1,0:T(8,128)(2,1)}), bf16[8,320,128]{2,1,0:T(8,128)(2,1)S(1)}, u32[]{:S(2)}, u32[]{:S(2)}) async-start(bf16[8,320,128]{2,1,0:T(8,128)(2,1)} %get-tuple-element.48), calls=%async_computation.1 | async-start | bytes 1310720 | tf_op jit(solution)/shard_map/all_to_all | solution.py:437
  84.1 14.3 %collective-permute-start = (bf16[16,64,256]{2,1,0:T(8,128)(2,1)S(1)}, bf16[16,64,256]{2,1,0:T(8,128)(2,1)S(1)}, u32[]{:S(2)}, u32[]{:S(2)}) collective-permute-start(bf16[16,64,256]{2,1,0:T(8,128)(2,1)S(1)} %copy-done.2), channel_id=1, source_target_pairs={{0,1},{1,2},{2,3},{3,0},{4,5},{5,6},{6,7},{7,4},{8,9},{9,10},{10,1... | collective-permute-start | bytes 1572872 | tf_op jit(solution)/shard_map/ppermute | solution.py:433
  85.0 25.5 %collective-permute-start.1 = (bf16[16,64,256]{2,1,0:T(8,128)(2,1)S(1)}, bf16[16,64,256]{2,1,0:T(8,128)(2,1)S(1)}, u32[]{:S(2)}, u32[]{:S(2)}) collective-permute-start(bf16[16,64,256]{2,1,0:T(8,128)(2,1)S(1)} %copy-done.2), channel_id=1, source_target_pairs={{0,2},{1,3},{2,0},{3,1},{4,6},{5,7},{6,4},{7,5},{8,10},{9,11},{10,... | collective-permute-start | bytes 1572872 | tf_op jit(solution)/shard_map/ppermute | solution.py:433
  87.7 22.8 %collective-permute-start.2 = (bf16[16,64,256]{2,1,0:T(8,128)(2,1)S(1)}, bf16[16,64,256]{2,1,0:T(8,128)(2,1)S(1)}, u32[]{:S(2)}, u32[]{:S(2)}) collective-permute-start(bf16[16,64,256]{2,1,0:T(8,128)(2,1)S(1)} %copy-done.2), channel_id=1, source_target_pairs={{0,3},{1,0},{2,1},{3,2},{4,7},{5,4},{6,5},{7,6},{8,11},{9,8},{10,9... | collective-permute-start | bytes 1572872 | tf_op jit(solution)/shard_map/ppermute | solution.py:433
  112.3 2.6 %collective-permute-start.17 = (bf16[512,256]{1,0:T(8,128)(2,1)S(1)}, bf16[512,256]{1,0:T(8,128)(2,1)S(1)}, u32[]{:S(2)}, u32[]{:S(2)}) collective-permute-start(bf16[512,256]{1,0:T(8,128)(2,1)S(1)} %get-tuple-element.53.own.cown), channel_id=1, source_target_pairs={{0,4},{4,0},{1,5},{5,1},{2,6},{6,2},{3,7},{7,3},{8,12},{12,8},{9,1... | collective-permute-start | bytes 786440 | tf_op jit(solution)/shard_map/ppermute | solution.py:441
  115.1 8.8 %collective-permute-start.18 = (bf16[512,256]{1,0:T(8,128)(2,1)S(1)}, bf16[512,256]{1,0:T(8,128)(2,1)S(1)}, u32[]{:S(2)}, u32[]{:S(2)}) collective-permute-start(bf16[512,256]{1,0:T(8,128)(2,1)S(1)} %shard_map.97.m0), channel_id=1, source_target_pairs={{0,8},{8,16},{16,24},{24,0},{1,9},{9,17},{17,25},{25,1},{2,10},{10... | collective-permute-start | bytes 786440 | tf_op jit(solution)/shard_map/ppermute | solution.py:433
  115.9 13.8 %collective-permute-start.19 = (bf16[512,256]{1,0:T(8,128)(2,1)S(1)}, bf16[512,256]{1,0:T(8,128)(2,1)S(1)}, u32[]{:S(2)}, u32[]{:S(2)}) collective-permute-start(bf16[512,256]{1,0:T(8,128)(2,1)S(1)} %shard_map.97.m0), channel_id=1, source_target_pairs={{0,16},{8,24},{16,0},{24,8},{1,17},{9,25},{17,1},{25,9},{2,18},{10... | collective-permute-start | bytes 786440 | tf_op jit(solution)/shard_map/ppermute | solution.py:433
  118.0 11.9 %collective-permute-start.20 = (bf16[512,256]{1,0:T(8,128)(2,1)S(1)}, bf16[512,256]{1,0:T(8,128)(2,1)S(1)}, u32[]{:S(2)}, u32[]{:S(2)}) collective-permute-start(bf16[512,256]{1,0:T(8,128)(2,1)S(1)} %shard_map.97.m0), channel_id=1, source_target_pairs={{0,24},{8,0},{16,8},{24,16},{1,25},{9,1},{17,9},{25,17},{2,26},{10... | collective-permute-start | bytes 786440 | tf_op jit(solution)/shard_map/ppermute | solution.py:433
  131.8 22.6 %all-to-all-start = ((bf16[8,256,128]{2,1,0:T(8,128)(2,1)}), bf16[8,256,128]{2,1,0:T(8,128)(2,1)S(1)}, u32[]{:S(2)}, u32[]{:S(2)}) async-start(bf16[8,256,128]{2,1,0:T(8,128)(2,1)} %get-tuple-element.54), calls=%async_computation | async-start | bytes 1048576 | tf_op jit(solution)/shard_map/all_to_all | solution.py:437
  138.4 3.5 %collective-permute-start.22 = (bf16[8,320,128]{2,1,0:T(8,128)(2,1)S(1)}, bf16[8,320,128]{2,1,0:T(8,128)(2,1)S(1)}, u32[]{:S(2)}, u32[]{:S(2)}) collective-permute-start(bf16[8,320,128]{2,1,0:T(8,128)(2,1)S(1)} %all-to-all-done.1.mine), channel_id=1, source_target_pairs={{0,4},{4,0},{1,5},{5,1},{2,6},{6,2},{3,7},{7,3},{8,12},{12,8},{9,1... | collective-permute-start | bytes 1966088 | tf_op jit(solution)/shard_map/ppermute | solution.py:441
  149.7 7.1 %collective-permute-start.23 = (bf16[64,256]{1,0:T(8,128)(2,1)S(1)}, bf16[64,256]{1,0:T(8,128)(2,1)S(1)}, u32[]{:S(2)}, u32[]{:S(2)}) collective-permute-start(bf16[64,256]{1,0:T(8,128)(2,1)S(1)} %get-tuple-element.62.own), channel_id=1, source_target_pairs={{0,4},{4,0},{1,5},{5,1},{2,6},{6,2},{3,7},{7,3},{8,12},{12,8},{9,1... | collective-permute-start | bytes 98312 | tf_op jit(solution)/shard_map/ppermute | solution.py:441
  154.4 16.3 %collective-permute-start.21 = (bf16[8,256,128]{2,1,0:T(8,128)(2,1)S(1)}, bf16[8,256,128]{2,1,0:T(8,128)(2,1)S(1)}, u32[]{:S(2)}, u32[]{:S(2)}) collective-permute-start(bf16[8,256,128]{2,1,0:T(8,128)(2,1)S(1)} %all-to-all-done.mine), channel_id=1, source_target_pairs={{0,4},{4,0},{1,5},{5,1},{2,6},{6,2},{3,7},{7,3},{8,12},{12,8},{9,1... | collective-permute-start | bytes 1572872 | tf_op jit(solution)/shard_map/ppermute | solution.py:441
  157.0 5.2 %collective-permute-start.24 = (f32[32,256]{1,0:T(8,128)S(1)}, f32[32,256]{1,0:T(8,128)S(1)}, u32[]{:S(2)}, u32[]{:S(2)}) collective-permute-start(f32[32,256]{1,0:T(8,128)S(1)} %shard_map.101.f0), channel_id=1, source_target_pairs={{0,8},{8,16},{16,24},{24,0},{1,9},{9,17},{17,25},{25,1},{2,10},{10... | collective-permute-start | bytes 98312 | tf_op jit(solution)/shard_map/ppermute | solution.py:433
  159.5 4.3 %collective-permute-start.25 = (f32[32,256]{1,0:T(8,128)S(1)}, f32[32,256]{1,0:T(8,128)S(1)}, u32[]{:S(2)}, u32[]{:S(2)}) collective-permute-start(f32[32,256]{1,0:T(8,128)S(1)} %shard_map.101.f0), channel_id=1, source_target_pairs={{0,16},{8,24},{16,0},{24,8},{1,17},{9,25},{17,1},{25,9},{2,18},{10... | collective-permute-start | bytes 98312 | tf_op jit(solution)/shard_map/ppermute | solution.py:433
  161.7 3.1 %collective-permute-start.26 = (f32[32,256]{1,0:T(8,128)S(1)}, f32[32,256]{1,0:T(8,128)S(1)}, u32[]{:S(2)}, u32[]{:S(2)}) collective-permute-start(f32[32,256]{1,0:T(8,128)S(1)} %shard_map.101.f0), channel_id=1, source_target_pairs={{0,24},{8,0},{16,8},{24,16},{1,25},{9,1},{17,9},{25,17},{2,26},{10... | collective-permute-start | bytes 98312 | tf_op jit(solution)/shard_map/ppermute | solution.py:433
  167.3 13.6 %all-to-all-start.2 = ((f32[8,32,256]{2,1,0:T(8,128)}), f32[8,32,256]{2,1,0:T(8,128)S(1)}, u32[]{:S(2)}, u32[]{:S(2)}) async-start(f32[8,32,256]{2,1,0:T(8,128)} %get-tuple-element.64), calls=%async_computation.2 | async-start | bytes 524288 | tf_op jit(solution)/shard_map/all_to_all | solution.py:437
  186.1 4.4 %collective-permute-start.27 = (bf16[8,32,128]{2,1,0:T(8,128)(2,1)S(1)}, bf16[8,32,128]{2,1,0:T(8,128)(2,1)S(1)}, u32[]{:S(2)}, u32[]{:S(2)}) collective-permute-start(bf16[8,32,128]{2,1,0:T(8,128)(2,1)S(1)} %get-tuple-element.68), channel_id=1, source_target_pairs={{0,1},{1,2},{2,3},{3,0},{4,5},{5,6},{6,7},{7,4},{8,9},{9,10},{10,1... | collective-permute-start | bytes 196616 | tf_op jit(solution)/shard_map/ppermute | solution.py:433
  186.7 5.0 %collective-permute-start.28 = (bf16[8,32,128]{2,1,0:T(8,128)(2,1)S(1)}, bf16[8,32,128]{2,1,0:T(8,128)(2,1)S(1)}, u32[]{:S(2)}, u32[]{:S(2)}) collective-permute-start(bf16[8,32,128]{2,1,0:T(8,128)(2,1)S(1)} %get-tuple-element.69), channel_id=1, source_target_pairs={{0,2},{1,3},{2,0},{3,1},{4,6},{5,7},{6,4},{7,5},{8,10},{9,11},{10,... | collective-permute-start | bytes 196616 | tf_op jit(solution)/shard_map/ppermute | solution.py:433
  189.4 3.1 %collective-permute-start.29 = (bf16[8,32,128]{2,1,0:T(8,128)(2,1)S(1)}, bf16[8,32,128]{2,1,0:T(8,128)(2,1)S(1)}, u32[]{:S(2)}, u32[]{:S(2)}) collective-permute-start(bf16[8,32,128]{2,1,0:T(8,128)(2,1)S(1)} %get-tuple-element.70), channel_id=1, source_target_pairs={{0,3},{1,0},{2,1},{3,2},{4,7},{5,4},{6,5},{7,6},{8,11},{9,8},{10,9... | collective-permute-start | bytes 196616 | tf_op jit(solution)/shard_map/ppermute | solution.py:433
  (14 other events, 86.4 us)
